TPU v7x, 32 devices: a whole 2x2x4 slice. The times are simulated.
32 devices in a mesh: dp: 16 (over z, y, core), owner: 2 (over x).
Axes of the slice: x: 2, y: 2, z: 4, core: 2. Of those that a mesh axis runs over, the one named last changes fastest.
Arguments:
- inputs: bfloat16 [2048, 8192], P('dp'), may hold values from -8 to 8
- out_grads: bfloat16 [2048, 1024], P('dp', 'owner'), may hold values from -12 to 12
- weights: float32 [32, 512, 512], P(('dp', 'owner')), may hold values from -0.0625 to 0.0625
- left_stats: float32 [32, 512, 512], P(('dp', 'owner')), as said below
- right_stats: float32 [32, 512, 512], P(('dp', 'owner')), as said below
- left_roots: float32 [32, 512, 512], P(('dp', 'owner')), as said below
- right_roots: float32 [32, 512, 512], P(('dp', 'owner')), as said below
- refresh: int32 [32], P(('dp', 'owner')), may hold values from 0 to 1, as said below
Outputs:
- new_left_stats: float32 [32, 512, 512], P(('dp', 'owner'))
- new_right_stats: float32 [32, 512, 512], P(('dp', 'owner'))
- new_left_roots: float32 [32, 512, 512], P(('dp', 'owner'))
- new_right_roots: float32 [32, 512, 512], P(('dp', 'owner'))
- update: float32 [32, 512, 512], P(('dp', 'owner'))
- queries: bfloat16 [2048, 1024], P('dp', 'owner')
Inputs may be any that keep to these rules, and one draw needn't show every extreme that they name: For every k, refresh[2k] + refresh[2k + 1] is at most 1, and refresh[0] + refresh[1] is 1. `left_stats`: every block is symmetric positive definite. `right_stats`: every block is symmetric positive definite. `left_roots`: every block is symmetric positive definite. `right_roots`: every block is symmetric positive definite.
All inputs are finite; a program needn't handle non-finite values.
Results may differ from a plain program's by a relative error of at most 0.015.
Values may be sent and summed in bfloat16 or wider, within the bound.
A program may use at most 128 MiB of HBM per device.

v0:
```python
import math

import jax
import jax.numpy as jnp
from jax import lax
from jax.sharding import PartitionSpec as P

NEWTON = 2


BETA = 0.95
DAMPING = 0.0001
HIGHEST = lax.Precision.HIGHEST


def matmul(left_mat, right_mat):
    return jnp.dot(left_mat, right_mat, precision=HIGHEST, preferred_element_type=jnp.float32)


def inverse_root(statistic):
    identity = jnp.eye(statistic.shape[0], dtype=jnp.float32)
    damped = statistic + DAMPING * identity
    factor_z = 2.5 / jnp.sqrt(jnp.sum(damped * damped))
    current = factor_z * damped
    result = jnp.sqrt(jnp.sqrt(factor_z)) * identity
    for turn in range(NEWTON):
        factor = 1.25 * identity - 0.25 * current
        result = matmul(result, factor)
        square = matmul(factor, factor)
        current = matmul(matmul(square, square), current)
    return result


def both_roots(left_stat, right_stat, left_old, right_old):
    return (inverse_root(left_stat), inverse_root(right_stat))


def stale_roots(left_stat, right_stat, left_old, right_old):
    return (left_old, right_old)


def body(inputs, out_grads, weights, left_stats, right_stats, left_roots, right_roots, refresh):
    tok_local, model_width = inputs.shape
    block_size = weights.shape[1]
    col_count = out_grads.shape[1]
    row_blocks = model_width // block_size
    col_blocks = col_count // block_size
    replicas = lax.axis_size("dp")
    tok_total = tok_local * replicas
    x_blocks = inputs.reshape(tok_local, row_blocks, block_size)
    g_blocks = out_grads.reshape(tok_local, col_blocks, block_size)
    feature_send = jnp.repeat(x_blocks, col_blocks, axis=1)
    grad_send = jnp.tile(g_blocks, (1, row_blocks, 1))
    feature_recv, grad_recv = (
        lax.all_to_all(feature_send, "dp", split_axis=1, concat_axis=1, tiled=True),
        lax.all_to_all(grad_send, "dp", split_axis=1, concat_axis=1, tiled=True),
    )
    group_size = 4

    def add_group(turn_index, running):
        x_group = lax.dynamic_slice_in_dim(feature_recv, turn_index * group_size, group_size, 1)
        g_group = lax.dynamic_slice_in_dim(grad_recv, turn_index * group_size, group_size, 1)
        products = (
            jnp.einsum("tsb,tsc->sbc", x_group, g_group, preferred_element_type=jnp.float32)
            / tok_total
        )
        products = lax.optimization_barrier(products.astype(jnp.bfloat16))
        return running + jnp.sum(products.astype(jnp.float32), 0)

    gradient = lax.fori_loop(
        0, replicas // group_size, add_group, jnp.zeros((block_size, block_size), jnp.float32)
    )
    left_new = BETA * left_stats[0] + (1.0 - BETA) * matmul(gradient, gradient.T)
    right_new = BETA * right_stats[0] + (1.0 - BETA) * matmul(gradient.T, gradient)
    refreshing = refresh[0] > 0
    left_root, right_root = lax.cond(
        refreshing, both_roots, stale_roots, left_new, right_new, left_roots[0], right_roots[0]
    )
    direction = matmul(matmul(left_root, gradient), right_root)
    direction = direction * (block_size / jnp.sqrt(jnp.sum(direction * direction) + 1e-12))
    rate = 0.25 / math.sqrt(model_width)
    updated = (weights[0] - rate * direction).astype(jnp.bfloat16)
    partial_out = jnp.einsum(
        "tsb,bc->tsc", feature_recv, updated, preferred_element_type=jnp.float32
    )
    returned = lax.all_to_all(
        partial_out.astype(jnp.bfloat16), "dp", split_axis=1, concat_axis=1, tiled=True
    ).astype(partial_out.dtype)
    queries = returned.reshape(tok_local, row_blocks, col_blocks, block_size).sum(1)
    queries = queries.reshape(tok_local, col_count).astype(jnp.bfloat16)
    return (
        left_new[None],
        right_new[None],
        left_root[None],
        right_root[None],
        direction[None],
        queries,
    )


def solution(mesh):
    in_specs = (
        P("dp", None),
        P("dp", "owner"),
        P(("dp", "owner"), None, None),
        P(("dp", "owner"), None, None),
        P(("dp", "owner"), None, None),
        P(("dp", "owner"), None, None),
        P(("dp", "owner"), None, None),
        P(("dp", "owner")),
    )
    out_specs = (
        P(("dp", "owner"), None, None),
        P(("dp", "owner"), None, None),
        P(("dp", "owner"), None, None),
        P(("dp", "owner"), None, None),
        P(("dp", "owner"), None, None),
        P("dp", "owner"),
    )
    return jax.shard_map(body, mesh=mesh, in_specs=in_specs, out_specs=out_specs, check_vma=False)
```

profile of v0, /device:TPU:15, one launch (start us, length us, event | category | flops | bytes accessed | tf_op | source)
XLA Modules:
  0.0 226.4 jit_solution(852852056815232677)
XLA Ops:
  0.6 2.3 copy.49
  2.9 3.2 %copy.22 = bf16[128,8192]{0,1:T(8,128)(2,1)S(1)} copy(bf16[128,8192]{1,0:T(8,128)(2,1)} %param.12) | data formatting | bytes 4194304 | tf_op args[0]
  6.1 2.6 %copy.23 = bf16[128,16,512]{2,0,1:T(8,128)(2,1)} copy(bf16[128,16,512]{0,2,1:T(8,128)(2,1)S(1)} %bitcast.47) | data formatting | bytes 4194304 | tf_op jit(solution)/shard_map/reshape;broadcast_in_dim;reshape | solution.py:52
  8.7 0.0 copy-start.13
  8.7 53.9 %all_to_all.15 = bf16[128,16,512]{2,0,1:T(8,128)(2,1)S(1)} all-to-all(bf16[128,16,512]{2,0,1:T(8,128)(2,1)} %copy.23), channel_id=1, replica_groups=mesh['dp'=16,'owner'=2] {'dp'}, dimensions={1} | all-to-all | bytes 4194304 | tf_op jit(solution)/shard_map/all_to_all | solution.py:55
  62.6 0.0 copy-done.13
  62.6 1.5 tile.2
  64.2 5.0 %all-to-all-start.1 = ((bf16[128,16,512]{2,0,1:T(8,128)(2,1)}), bf16[128,16,512]{2,0,1:T(8,128)(2,1)}, u32[]{:S(2)}, u32[]{:S(2)}) async-start(bf16[128,16,512]{2,0,1:T(8,128)(2,1)} %tile.2), calls=%async_computation.1 | async-start | bytes 4194304 | tf_op jit(solution)/shard_map/all_to_all | solution.py:56
  69.9 46.9 %all-to-all-done.1 = bf16[128,16,512]{2,0,1:T(8,128)(2,1)} async-done(((bf16[128,16,512]{2,0,1:T(8,128)(2,1)}), bf16[128,16,512]{2,0,1:T(8,128)(2,1)}, u32[]{:S(2)}, u32[]{:S(2)}) %all-to-all-start.1) | async-done | bytes 2097184 | tf_op jit(solution)/shard_map/all_to_all | solution.py:56
  116.7 10.0 %while.14 = (s32[]{:T(128)}, f32[512,512]{1,0:T(8,128)S(1)}, bf16[128,16,512]{2,0,1:T(8,128)(2,1)S(1)}, bf16[128,16,512]{2,0,1:T(8,128)(2,1)}, s32[]{:T(128)}, /*index=5*/s32[]{:T(128)}, s32[]{:T(128)}, s32[]{:T(128)}) while((s32[]{:T(128)}, f32[512,512]{1,0:T(8,128)S(1)}, bf16[128,16,512]{2,0,1:T(8,128)(2,1)S(1)}, ...), condition=%wide.region_2.0_spmd.clone, body=%wide.region_0.0_spmd.clone.sunk | while | flops 272891904 | bytes 9438357 | solution.py:70
  116.7 1.8 multiply_convert_fusion.2
  118.5 0.3 convert_reduce_fusion.2
  118.8 0.4 select_add_fusion.10
  119.2 1.8 multiply_convert_fusion.2
  121.0 0.3 convert_reduce_fusion.2
  121.4 0.4 select_add_fusion.10
  121.7 1.8 multiply_convert_fusion.2
  123.6 0.3 convert_reduce_fusion.2
  123.9 0.4 select_add_fusion.10
  124.3 1.8 multiply_convert_fusion.2
  126.1 0.3 convert_reduce_fusion.2
  126.4 0.4 select_add_fusion.10
  126.8 0.0 copy-start.3
  126.8 1.3 copy-done.3
  128.1 0.0 copy-start.12
  128.1 3.2 %fusion.51 = f32[512,512]{1,0:T(8,128)S(1)} fusion(f32[512,512]{1,0:T(8,128)S(1)} %get-tuple-element.107, f32[1,512,512]{2,1,0:T(8,128)} %param.16), kind=kOutput, calls=%fused_computation.67 | convolution fusion | flops 1611399168 | bytes 3145728 | tf_op jit(solution)/shard_map/dot_general | solution.py:17
  131.3 0.0 copy-done.12
  131.3 0.0 copy-start.4
  131.3 0.0 copy-start.2
  131.4 1.9 fusion.52
  133.3 0.0 copy-start.7
  133.3 0.0 copy-done.2
  133.3 1.0 copy-done.7
  134.2 0.0 copy-done.4
  134.2 2.2 conditional.1
  134.2 1.2 copy.38
  135.5 1.0 copy.39
  136.4 0.0 copy-start.11
  136.4 1.0 copy-done.11
  137.4 3.1 %fusion.63 = f32[512,512]{1,0:T(8,128)S(1)} fusion(f32[512,512]{1,0:T(8,128)} %get-tuple-element.110, f32[512,512]{1,0:T(8,128)S(1)} %get-tuple-element.107), kind=kOutput, calls=%fused_computation.82 | convolution fusion | flops 1610612736 | bytes 3145728 | tf_op jit(solution)/shard_map/dot_general | solution.py:17
  140.5 0.0 copy-start.14
  140.5 2.6 %multiply_reduce_fusion.2 = (f32[]{:T(128)}, f32[512,512]{1,0:T(8,128)S(1)}) fusion(f32[512,512]{1,0:T(8,128)S(1)} %fusion.63, f32[512,512]{1,0:T(8,128)S(1)} %get-tuple-element.111), kind=kOutput, calls=%fused_computation.72 | convolution fusion | flops 1611137024 | bytes 3145732 | tf_op jit(solution)/shard_map/dot_general | solution.py:17
  143.7 0.0 copy-done.14
  143.8 4.2 %convert_bitcast_fusion = bf16[128,16,512]{0,2,1:T(8,128)(2,1)} fusion(bf16[128,16,512]{2,0,1:T(8,128)(2,1)} %copy-done.3, f32[512,512]{1,0:T(8,128)S(1)} %get-tuple-element.160, f32[1,512,512]{2,1,0:T(8,128)S(1)} %copy-done.14, f32[]{:T(128)S(6)} %div.14), kind=kOutput, calls=%fused_computation.65 | convolution fusion | flops 1075838976 | bytes 6291460 | tf_op jit(solution)/shard_map/tsb,bc->tsc/dot_general | solution.py:83
  148.0 30.0 %all-to-all-start.2 = ((bf16[128,16,512]{0,2,1:T(8,128)(2,1)}), bf16[128,16,512]{0,2,1:T(8,128)(2,1)S(1)}, u32[]{:S(2)}, u32[]{:S(2)}) async-start(bf16[128,16,512]{0,2,1:T(8,128)(2,1)} %convert_bitcast_fusion), calls=%async_computation.2 | async-start | bytes 4194304 | tf_op jit(solution)/shard_map/all_to_all | solution.py:86
  178.0 1.1 multiply_bitcast_fusion
  179.0 46.4 %all-to-all-done.2 = bf16[128,16,512]{0,2,1:T(8,128)(2,1)S(1)} async-done(((bf16[128,16,512]{0,2,1:T(8,128)(2,1)}), bf16[128,16,512]{0,2,1:T(8,128)(2,1)S(1)}, u32[]{:S(2)}, u32[]{:S(2)}) %all-to-all-start.2) | async-done | bytes 2097184 | tf_op jit(solution)/shard_map/all_to_all | solution.py:86
  225.4 0.3 reduce_sum.53
  225.7 0.8 copy.26
  (1 shorter events, 0.0 us)
Async XLA Ops:
  8.7 53.9 %copy-start.13 = (bf16[128,512]{1,0:T(8,128)(2,1)S(1)}, bf16[128,512]{1,0:T(8,128)(2,1)}, u32[]{:S(2)}) copy-start(bf16[128,512]{1,0:T(8,128)(2,1)} %param.13) | copy-start | bytes 393220
  64.2 52.5 %all-to-all-start.1 = ((bf16[128,16,512]{2,0,1:T(8,128)(2,1)}), bf16[128,16,512]{2,0,1:T(8,128)(2,1)}, u32[]{:S(2)}, u32[]{:S(2)}) async-start(bf16[128,16,512]{2,0,1:T(8,128)(2,1)} %tile.2), calls=%async_computation.1 | async-start | bytes 4194304 | tf_op jit(solution)/shard_map/all_to_all | solution.py:56
  126.8 1.3 copy-start.3
  128.1 3.2 %copy-start.12 = (f32[1,512,512]{2,1,0:T(8,128)S(1)}, f32[1,512,512]{2,1,0:T(8,128)}, u32[]{:S(2)}) copy-start(f32[1,512,512]{2,1,0:T(8,128)} %param.15) | copy-start | bytes 3145732
  131.3 2.9 %copy-start.4 = (f32[512,512]{1,0:T(8,128)}, f32[512,512]{1,0:T(8,128)S(1)}, u32[]{:S(2)}) copy-start(f32[512,512]{1,0:T(8,128)S(1)} %fusion.51) | copy-start | bytes 3145732
  131.3 1.9 copy-start.2
  133.3 1.0 copy-start.7
  136.4 1.0 copy-start.11
  140.5 3.3 %copy-start.14 = (f32[1,512,512]{2,1,0:T(8,128)S(1)}, f32[1,512,512]{2,1,0:T(8,128)}, u32[]{:S(2)}) copy-start(f32[1,512,512]{2,1,0:T(8,128)} %param.14) | copy-start | bytes 3145732
  148.0 77.4 %all-to-all-start.2 = ((bf16[128,16,512]{0,2,1:T(8,128)(2,1)}), bf16[128,16,512]{0,2,1:T(8,128)(2,1)S(1)}, u32[]{:S(2)}, u32[]{:S(2)}) async-start(bf16[128,16,512]{0,2,1:T(8,128)(2,1)} %convert_bitcast_fusion), calls=%async_computation.2 | async-start | bytes 4194304 | tf_op jit(solution)/shard_map/all_to_all | solution.py:86
where the time goes:
time: 227 us; the launch traced here: 226 us
  waiting for transfers between devices  93.2 us (41%)
  blocking collectives  53.9 us (24%)
  starting transfers between devices  35 us (15%)
  matrix products  22.2 us (10%)
  local copies, waits for them, and re-layouts  15.9 us (7%)
  other arithmetic  4.05 us (2%)
    all_to_all x1, blocking collectives, body(): lax.all_to_all(feature_send, 'dp', split_axis=1, concat_axis=1, tiled=True)  53.9 us
    all_to_all x1, waiting for transfers between devices, body(): lax.all_to_all(grad_send, 'dp', split_axis=1, concat_axis=1, tiled=True)  46.9 us
    all_to_all x1, waiting for transfers between devices, body(): lax.all_to_all(partial_out.astype(jnp.bfloat16), 'dp', split_axis=1, conc...  46.4 us
    all_to_all x1, starting transfers between devices, body(): lax.all_to_all(partial_out.astype(jnp.bfloat16), 'dp', split_axis=1, conc...  30 us
    dot_general x4, matrix products, matmul(): jnp.dot(left_mat, right_mat, precision=HIGHEST, preferred_element_type=jn...  10.7 us
    unnamed x19, local copies, waits for them, and re-layouts  9.53 us
    dot_general x4, matrix products, add_group(): jnp.einsum('tsb,tsc->sbc', x_group, g_group, preferred_element_type=jnp.f...  7.2 us
    all_to_all x1, starting transfers between devices, body(): lax.all_to_all(grad_send, 'dp', split_axis=1, concat_axis=1, tiled=True)  5.02 us
  transfers between devices with their start and end apart: 2, of which 2 were waited for; matrix products, arithmetic and copies ran while one was open for 0% of the time, Pallas kernels for 0%

commit v1 on v0

v1 whole, which is shorter than its diff:
```python
import math

import jax
import jax.numpy as jnp
from jax import lax
from jax.sharding import PartitionSpec as P

BETA = 0.95
DAMPING = 0.0001
BF16 = jnp.bfloat16
F32 = jnp.float32


def dot(a, b, dims=((1,), (0,))):
    return lax.dot_general(a.astype(BF16), b.astype(BF16), (dims, ((), ())), preferred_element_type=F32)


def split(a):
    high = a.astype(BF16)
    return high, (a - high.astype(F32)).astype(BF16)


def dot3(a, b):
    a_high, a_low = split(a)
    b_high, b_low = split(b)
    return dot(a_high, b_high) + (dot(a_high, b_low) + dot(a_low, b_high))


def inverse_root(statistic):
    eye = jnp.eye(statistic.shape[0], dtype=F32)
    damped = statistic + DAMPING * eye
    z = 2.5 / jnp.sqrt(jnp.sum(damped * damped))
    m = z * damped
    p = dot(m, m)
    r = 1.5625 * m - 0.625 * p + 0.0625 * dot(p, m)
    w = 0.0625 * r + 0.1953125 * m - 0.01953125 * p
    return jnp.sqrt(jnp.sqrt(z)) * (1.5625 * eye - 0.3125 * m - 0.48828125 * r + dot(w, r))


def roots(left_stat, right_stat, left_old, right_old):
    return (inverse_root(left_stat), inverse_root(right_stat))


def stale(left_stat, right_stat, left_old, right_old):
    return (left_old, right_old)


def body(inputs, out_grads, weights, left_stats, right_stats, left_roots, right_roots, refresh):
    tok_local, model_width = inputs.shape
    block = weights.shape[1]
    col_count = out_grads.shape[1]
    row_blocks = model_width // block
    col_blocks = col_count // block
    replicas = lax.axis_size("dp")
    tok_total = tok_local * replicas
    mine = lax.axis_index("dp") % col_blocks
    grads = lax.all_gather(out_grads, "dp", axis=0, tiled=True)
    grads = lax.dynamic_slice_in_dim(grads, mine * block, block, 1)
    send = jnp.repeat(inputs.reshape(tok_local, row_blocks, block).transpose(1, 0, 2), col_blocks, axis=0)
    features = lax.all_to_all(send, "dp", split_axis=0, concat_axis=0, tiled=True)
    features = features.reshape(tok_total, block)
    gradient = dot(features, grads, ((0,), (0,))) / tok_total
    left_new = BETA * left_stats[0] + (1.0 - BETA) * dot(gradient, gradient, ((1,), (1,)))
    right_new = BETA * right_stats[0] + (1.0 - BETA) * dot(gradient, gradient, ((0,), (0,)))
    left_root, right_root = lax.cond(
        refresh[0] > 0, roots, stale, left_new, right_new, left_roots[0], right_roots[0]
    )
    direction = dot3(dot3(left_root, gradient), right_root)
    direction = direction * (block / jnp.sqrt(jnp.sum(direction * direction) + 1e-12))
    rate = 0.25 / math.sqrt(model_width)
    updated = (weights[0] - rate * direction).astype(BF16)
    partial = dot(features, updated).astype(BF16)
    if col_blocks > 1:
        partial = lax.dynamic_update_slice(jnp.zeros((tok_total, col_count), BF16), partial, (0, mine * block))
    queries = lax.psum_scatter(partial, "dp", scatter_dimension=0, tiled=True)
    return (left_new[None], right_new[None], left_root[None], right_root[None], direction[None], queries)


def solution(mesh):
    blocks = P(("dp", "owner"), None, None)
    in_specs = (P("dp", None), P("dp", "owner"), blocks, blocks, blocks, blocks, blocks, P(("dp", "owner")))
    out_specs = (blocks,) * 5 + (P("dp", "owner"),)
    return jax.shard_map(body, mesh=mesh, in_specs=in_specs, out_specs=out_specs, check_vma=False)
```

time: 227 us -> 188 us (0.83)
  the two profiles are of different devices: /device:TPU:15 before, /device:TPU:2 now
where the time goes in v1:
time: 188 us; the launch traced here: 186 us
  waiting for transfers between devices  120 us (64%)
  matrix products  21.1 us (11%)
  local copies, waits for them, and re-layouts  19.5 us (10%)
  between operations  15.5 us (8%)
  starting transfers between devices  6.02 us (3%)
  other arithmetic  1.95 us (1%)
    unnamed x3, waiting for transfers between devices  62.7 us
    all_to_all x1, waiting for transfers between devices, body(): lax.all_to_all(send, 'dp', split_axis=0, concat_axis=0, tiled=True)  43.8 us
    dot_general x16, matrix products, dot(): lax.dot_general(a.astype(BF16), b.astype(BF16), (dims, ((), ())), preferr...  21.1 us
    unnamed x31, local copies, waits for them, and re-layouts  16.9 us
    all_gather x1, waiting for transfers between devices, body(): grads = lax.all_gather(out_grads, 'dp', axis=0, tiled=True)  13.8 us
    all_to_all x1, starting transfers between devices, body(): lax.all_to_all(send, 'dp', split_axis=0, concat_axis=0, tiled=True)  5.94 us
  transfers between devices with their start and end apart: 3, of which 3 were waited for; matrix products, arithmetic and copies ran while one was open for 2% of the time, Pallas kernels for 0%

profile of v1, /device:TPU:2, one launch (start us, length us, event | category | flops | bytes accessed | tf_op | source)
XLA Modules:
  0.0 185.9 jit_solution(11782345816067981194)
XLA Ops:
  7.2 0.0 copy-start.10
  7.2 2.4 %copy.40 = f32[1,512,512]{2,1,0:T(8,128)} copy(f32[1,512,512]{2,1,0:T(8,128)} %param.16) | data formatting | bytes 2097152
  9.6 0.0 copy-done.10
  9.6 2.4 %copy.21 = bf16[128,8192]{0,1:T(8,128)(2,1)} copy(bf16[128,8192]{1,0:T(8,128)(2,1)S(1)} %copy-done.10) | data formatting | bytes 4194304 | tf_op args[0]
  12.0 5.9 %all-to-all-start = ((bf16[16,128,512]{1,2,0:T(8,128)(2,1)}), bf16[16,128,512]{1,2,0:T(8,128)(2,1)S(1)}, u32[]{:S(2)}, u32[]{:S(2)}) async-start(bf16[16,128,512]{1,2,0:T(8,128)(2,1)} %bitcast.40), calls=%async_computation | async-start | bytes 4194304 | tf_op jit(solution)/shard_map/all_to_all | solution.py:60
  18.0 0.0 all-gather.2.cloned.1.call-start
  18.0 0.7 all-gather.2.cloned.1.call-update
  18.7 0.0 reduce-scatter.4.cloned.1.call-start
  19.4 43.8 %all-to-all-done = bf16[16,128,512]{1,2,0:T(8,128)(2,1)S(1)} async-done(((bf16[16,128,512]{1,2,0:T(8,128)(2,1)}), bf16[16,128,512]{1,2,0:T(8,128)(2,1)S(1)}, u32[]{:S(2)}, u32[]{:S(2)}) %all-to-all-start) | async-done | bytes 2097184 | tf_op jit(solution)/shard_map/all_to_all | solution.py:60
  63.2 2.6 %copy.22 = bf16[16,128,512]{2,1,0:T(8,128)(2,1)} copy(bf16[16,128,512]{1,2,0:T(8,128)(2,1)S(1)} %all-to-all-done) | data formatting | bytes 4194304 | tf_op jit(solution)/shard_map/all_to_all | solution.py:60
  65.8 13.8 %all-gather.2.cloned.1.call-done = bf16[2048,512]{1,0:T(8,128)(2,1)} async-done(((bf16[128,512]{1,0:T(8,128)(2,1)}), bf16[2048,512]{1,0:T(8,128)(2,1)}) %all-gather.2.cloned.1.call-update) | async-done | bytes 2097168 | tf_op jit(solution)/shard_map/all_gather | solution.py:57
  79.6 0.0 copy-start.11
  79.6 4.6 %fusion.87 = (bf16[512,512]{1,0:T(8,128)(2,1)S(1)}, f32[512,512]{1,0:T(8,128)}) fusion(bf16[2048,512]{1,0:T(8,128)(2,1)} %bitcast.41, bf16[2048,512]{1,0:T(8,128)(2,1)} %all-gather.2.cloned.1.call-done), kind=kOutput, calls=%fused_computation.106 | convolution fusion | flops 1074266112 | bytes 5767168 | tf_op jit(solution)/shard_map/dot_general | solution.py:15
  84.1 0.0 copy-start.12
  84.1 0.0 copy-done.11
  84.1 0.5 fusion.67
  84.6 0.7 copy-done.12
  85.3 0.0 copy-start.4
  85.3 0.0 copy-start.2
  85.4 0.5 fusion.68
  85.8 0.0 copy-start.5
  85.8 1.5 copy-done.2
  87.3 0.0 copy-done.4
  87.3 0.0 copy-done.5
  87.3 11.7 %conditional.2 = (f32[512,512]{1,0:T(8,128)S(1)}, f32[512,512]{1,0:T(8,128)}, f32[1,512,512]{2,1,0:T(8,128)}, f32[1,512,512]{2,1,0:T(8,128)}) conditional(s32[]{:T(128)} %bitcast.11, (f32[1,512,512]{2,1,0:T(8,128)S(1)}, f32[1,512,512]{2,1,0:T(8,128)}) %tuple.58, (f32[512,512]{1,0:T(8,128)S(1)}, f32[512,512]{1,0:T(8,128)S(1)}) %tuple.31), branch_computations={%region_0.1_spmd.clone, %region_1.4_spmd.clone} | conditional | flops 1634729984 | bytes 46137628
  87.3 0.0 copy-start.6
  87.3 1.0 copy-done.6
  88.3 0.9 multiply_reduce_fusion
  89.2 0.0 copy-start.7
  90.7 0.5 fusion.16
  91.2 0.0 copy-done.7
  91.2 0.5 fusion.11
  91.7 0.0 copy-start.8
  91.7 0.5 fusion.3
  92.2 0.7 copy-done.8
  92.9 0.6 fusion.2
  93.5 0.0 copy-start
  93.5 1.0 copy.32
  94.5 0.5 fusion.1
  95.0 0.0 copy-done
  95.0 1.6 fusion
  96.7 0.0 copy-start.1
  96.7 2.4 %copy.33 = f32[1,512,512]{2,1,0:T(8,128)} copy(f32[1,512,512]{2,1,0:T(8,128)} %bitcast.20) | data formatting | bytes 2097152
  99.0 0.0 copy-done.1
  99.0 0.0 copy-start.9
  99.0 0.4 fusion.80
  99.5 0.8 copy-done.9
  100.2 0.4 fusion.70
  100.7 0.5 fusion.66
  101.2 2.0 %fusion.71 = f32[512,512]{1,0:T(8,128)S(1)} fusion(f32[512,512]{1,0:T(8,128)} %get-tuple-element.81, f32[512,512]{1,0:T(8,128)S(1)} %fusion.66), kind=kOutput, calls=%fused_computation.91 | convolution fusion | flops 269746176 | bytes 3145728 | tf_op jit(solution)/shard_map/dot_general | solution.py:15
  103.2 1.7 fusion.76
  104.8 0.0 copy-start.3
  104.8 2.6 %multiply_reduce_fusion.2 = (f32[]{:T(128)}, f32[512,512]{1,0:T(8,128)S(1)}) fusion(f32[512,512]{1,0:T(8,128)S(1)} %fusion.76, f32[512,512]{1,0:T(8,128)S(1)} %fusion.71, f32[512,512]{1,0:T(8,128)} %get-tuple-element.81, f32[512,512]{1,0:T(8,128)S(1)} %fusion.66), kind=kOutput, calls=%fused_computation.84 | convolution fusion | flops 270794752 | bytes 5242884 | tf_op jit(solution)/shard_map/dot_general | solution.py:15
  108.1 0.0 copy-done.3
  108.1 3.9 %fusion.64 = bf16[2048,512]{0,1:T(8,128)(2,1)} fusion(bf16[2048,512]{1,0:T(8,128)(2,1)S(1)} %bitcast.42, f32[1,512,512]{2,1,0:T(8,128)} %param.12, f32[512,512]{1,0:T(8,128)S(1)} %get-tuple-element.99, f32[]{:T(128)S(6)} %div.17), kind=kOutput, calls=%fused_computation.72 | convolution fusion | flops 1075838976 | bytes 6291460 | tf_op jit(solution)/shard_map/dot_general | solution.py:15
  112.0 3.9 %copy.24 = bf16[2048,512]{1,0:T(8,128)(2,1)} copy(bf16[2048,512]{0,1:T(8,128)(2,1)} %fusion.64) | data formatting | bytes 4194304
  115.9 0.0 reduce-scatter.4.cloned.1.call-update
  115.9 1.1 multiply_bitcast_fusion
  117.0 62.0 %reduce-scatter.4.cloned.1.call-done = bf16[128,512]{1,0:T(8,128)(2,1)} async-done(((bf16[2048,512]{1,0:T(8,128)(2,1)}), bf16[128,512]{1,0:T(8,128)(2,1)}) %reduce-scatter.4.cloned.1.call-update) | async-done | bytes 131088
Async XLA Ops:
  7.2 2.4 %copy-start.10 = (bf16[128,8192]{1,0:T(8,128)(2,1)S(1)}, bf16[128,8192]{1,0:T(8,128)(2,1)}, u32[]{:S(2)}) copy-start(bf16[128,8192]{1,0:T(8,128)(2,1)} %param.10) | copy-start | bytes 6291460
  12.0 51.1 %all-to-all-start = ((bf16[16,128,512]{1,2,0:T(8,128)(2,1)}), bf16[16,128,512]{1,2,0:T(8,128)(2,1)S(1)}, u32[]{:S(2)}, u32[]{:S(2)}) async-start(bf16[16,128,512]{1,2,0:T(8,128)(2,1)} %bitcast.40), calls=%async_computation | async-start | bytes 4194304 | tf_op jit(solution)/shard_map/all_to_all | solution.py:60
  18.0 61.6 %all-gather.2.cloned.1.call-start = ((), (), s32[]{:S(2)}) async-start(), calls=%async_computation.2 | async-start | bytes 2228224 | tf_op jit(solution)/shard_map/all_gather | solution.py:57
  18.7 160.3 %reduce-scatter.4.cloned.1.call-start = ((), (), s32[]{:S(2)}) async-start(), calls=%async_computation.3 | async-start | bytes 2228224
  79.6 4.6 %copy-start.11 = (f32[1,512,512]{2,1,0:T(8,128)S(1)}, f32[1,512,512]{2,1,0:T(8,128)}, u32[]{:S(2)}) copy-start(f32[1,512,512]{2,1,0:T(8,128)} %param.14) | copy-start | bytes 3145732
  84.1 1.2 copy-start.12
  85.3 2.0 %copy-start.4 = (f32[512,512]{1,0:T(8,128)}, f32[512,512]{1,0:T(8,128)S(1)}, u32[]{:S(2)}) copy-start(f32[512,512]{1,0:T(8,128)S(1)} %fusion.67) | copy-start | bytes 3145732
  85.3 2.0 %copy-start.2 = (f32[1,512,512]{2,1,0:T(8,128)S(1)}, f32[1,512,512]{2,1,0:T(8,128)}, u32[]{:S(2)}) copy-start(f32[1,512,512]{2,1,0:T(8,128)} %param.15) | copy-start | bytes 3145732
  85.8 1.5 copy-start.5
  87.3 1.0 copy-start.6
  89.2 2.0 %copy-start.7 = (f32[512,512]{1,0:T(8,128)S(1)}, f32[512,512]{1,0:T(8,128)}, u32[]{:S(2)}) copy-start(f32[512,512]{1,0:T(8,128)} %copy-done.6) | copy-start | bytes 3145732
  91.7 1.2 copy-start.8
  93.5 1.5 copy-start
  96.7 2.4 %copy-start.1 = (f32[512,512]{1,0:T(8,128)S(1)}, f32[512,512]{1,0:T(8,128)}, u32[]{:S(2)}) copy-start(f32[512,512]{1,0:T(8,128)} %copy-done) | copy-start | bytes 3145732
  99.0 1.2 copy-start.9
  104.8 3.3 %copy-start.3 = (bf16[16,128,512]{2,1,0:T(8,128)(2,1)S(1)}, bf16[16,128,512]{2,1,0:T(8,128)(2,1)}, u32[]{:S(2)}) copy-start(bf16[16,128,512]{2,1,0:T(8,128)(2,1)} %copy.22) | copy-start | bytes 6291460
Sparse Core Ops, SparseCore 0:
  21.0 58.5 all-gather.1
  116.1 62.9 reduce-scatter.3

commit v2 on v1

--- a/solution.py
+++ b/solution.py
@@ -1,8 +1,11 @@
+import functools
 import math
 
 import jax
 import jax.numpy as jnp
 from jax import lax
+from jax.experimental import pallas as pl
+from jax.experimental.pallas import tpu as pltpu
 from jax.sharding import PartitionSpec as P
 
 BETA = 0.95
@@ -44,6 +47,187 @@
 def stale(left_stat, right_stat, left_old, right_old):
     return (left_old, right_old)
 
+LINE = 4
+
+
+def flip(index, stride):
+    return index + stride - 2 * stride * lax.rem(lax.div(index, stride), 2)
+
+
+def remote(src, dst, send, recv, peer):
+    return pltpu.make_async_remote_copy(
+        src_ref=src, dst_ref=dst, send_sem=send, recv_sem=recv,
+        device_id=peer, device_id_type=pl.DeviceIdType.MESH,
+    )
+
+
+def greet(peers):
+    barrier = pltpu.get_barrier_semaphore()
+    for peer in peers:
+        pl.semaphore_signal(barrier, inc=1, device_id=peer, device_id_type=pl.DeviceIdType.MESH)
+    pl.semaphore_wait(barrier, len(peers))
+
+
+def by_distance(n):
+    return sorted(range(1, n), key=lambda k: -min(k, n - k))
+
+
+def gather_kernel(n, x_ref, g_ref, f_ref, ga_ref, x_own, g_own, own, fs, fr, xs, xr, zs, zr, ys, yr, cs, cr):
+    me, mine = lax.axis_index("dp"), lax.axis_index("owner")
+    nz = n // LINE
+    rows, width = g_ref.shape
+    half = rows // 2
+    near = pl.ds(pl.multiple_of(mine * half, half), half)
+    far = pl.ds(pl.multiple_of((1 - mine) * half, half), half)
+    pair, row = flip(me, 1), flip(me, 2)
+
+    def cols(block):
+        return pl.ds(pl.multiple_of(block * width, width), width)
+
+    own_in = [
+        pltpu.make_async_copy(x_ref.at[:, cols(me)], x_own, own.at[0]),
+        pltpu.make_async_copy(g_ref, g_own, own.at[1]),
+    ]
+    for copy in own_in:
+        copy.start()
+    greet([(lax.rem(me + k, n), mine) for k in range(1, n)] + [(me, 1 - mine)])
+    sent = []
+
+    def go(copy):
+        copy.start()
+        sent.append(copy)
+        return copy
+
+    z_copy = {}
+    for k in by_distance(nz):
+        z_copy[k] = go(remote(g_ref, ga_ref.at[me], zs.at[k], zr.at[k], (lax.rem(me + LINE * k, n), mine)))
+    f_copy = {}
+    order = by_distance(n)
+    for k in order:
+        peer = lax.rem(me + k, n)
+        f_copy[k] = go(remote(x_ref.at[near, cols(peer)], f_ref.at[me, near], fs.at[k], fr.at[k], (peer, mine)))
+    y_copy, c_copy = {}, {}
+    for k in [0] + by_distance(nz):
+        source = lax.rem(me - LINE * k + n, n)
+        if k:
+            z_copy[k].wait_recv()
+        block = ga_ref.at[source] if k else g_ref
+        y_copy[k] = go(remote(block, ga_ref.at[source], ys.at[k], yr.at[k], (row, mine)))
+        c_copy[k] = go(remote(block, ga_ref.at[source], cs.at[k], cr.at[k], (pair, mine)))
+    own_out = [
+        pltpu.make_async_copy(x_own, f_ref.at[me], own.at[2]),
+        pltpu.make_async_copy(g_own, ga_ref.at[me], own.at[3]),
+    ]
+    for first, second in zip(own_in, own_out):
+        first.wait()
+        second.start()
+    x_copy = {}
+
+    def pass_on(k):
+        f_copy[k].wait_recv()
+        held = f_ref.at[lax.rem(me - k + n, n), near]
+        x_copy[k] = go(remote(held, held, xs.at[k], xr.at[k], (me, 1 - mine)))
+
+    quick = order[::-1]
+    for at, k in enumerate([0] + by_distance(nz)):
+        y_copy[k].wait_recv()
+        source = lax.rem(row - LINE * k + n, n)
+        block = ga_ref.at[source]
+        c_copy[nz + k] = go(remote(block, block, cs.at[nz + k], cr.at[nz + k], (pair, mine)))
+    for k in quick:
+        pass_on(k)
+    for k in range(2 * nz):
+        c_copy[k].wait_recv()
+    for k in quick:
+        x_copy[k].wait_recv()
+    for copy in own_out:
+        copy.wait()
+    for copy in sent:
+        copy.wait_send()
+
+
+def gather(n, inputs, out_grads):
+    rows, width = out_grads.shape
+    nz = n // LINE
+    dma = pltpu.SemaphoreType.DMA
+    anywhere = pl.BlockSpec(memory_space=pl.ANY)
+    return pl.pallas_call(
+        functools.partial(gather_kernel, n),
+        out_shape=[jax.ShapeDtypeStruct((n, rows, width), BF16)] * 2,
+        in_specs=[anywhere] * 2,
+        out_specs=[anywhere] * 2,
+        scratch_shapes=[pltpu.VMEM((rows, width), BF16)] * 2
+        + [dma((4,))] + [dma((n,))] * 4 + [dma((nz,))] * 4 + [dma((2 * nz,))] * 2,
+        compiler_params=pltpu.CompilerParams(collective_id=0, has_side_effects=True),
+        name="gather_blocks",
+    )(inputs, out_grads)
+
+
+def reduce_kernel(n, f_ref, w_ref, q_ref, a_out, a_in, b_out, b_in, c_out, c_in, total, a_s, a_r, b_s, b_r, c_s, c_r):
+    me, mine = lax.axis_index("dp"), lax.axis_index("owner")
+    nz = n // LINE
+    pair, row = flip(me, 1), flip(me, 2)
+    order = by_distance(nz) + [0]
+    greet([(pair, mine), (row, mine)] + [(lax.rem(me + LINE * k, n), mine) for k in range(1, nz)])
+
+    def part(block):
+        return jnp.dot(f_ref[block], w_ref[...], preferred_element_type=F32)
+
+    sent = []
+
+    def go(copy):
+        copy.start()
+        sent.append(copy)
+        return copy
+
+    a_copy, b_copy, c_copy = {}, {}, {}
+    for k in order:
+        for turn, base in ((1, flip(row, 1)), (0, pair)):
+            at = 2 * k + turn
+            a_out[at] = part(lax.rem(base + LINE * k, n)).astype(BF16)
+            a_copy[at] = go(remote(a_out.at[at], a_in.at[at], a_s.at[at], a_r.at[at], (pair, mine)))
+    for k in order:
+        mine_part = part(lax.rem(row + LINE * k, n))
+        a_copy[2 * k + 1].wait_recv()
+        b_out[k] = (mine_part + a_in[2 * k + 1].astype(F32)).astype(BF16)
+        b_copy[k] = go(remote(b_out.at[k], b_in.at[k], b_s.at[k], b_r.at[k], (row, mine)))
+    for k in order:
+        total[k] = part(lax.rem(me + LINE * k, n))
+        a_copy[2 * k].wait_recv()
+        total[k] += a_in[2 * k].astype(F32)
+    for k in order:
+        b_copy[k].wait_recv()
+        if k:
+            c_out[k] = (total[k] + b_in[k].astype(F32)).astype(BF16)
+            peer = lax.rem(me + LINE * k, n)
+            c_copy[k] = go(remote(c_out.at[k], c_in.at[k], c_s.at[k], c_r.at[k], (peer, mine)))
+    result = total[0] + b_in[0].astype(F32)
+    for k in by_distance(nz)[::-1]:
+        c_copy[k].wait_recv()
+        result = result + c_in[k].astype(F32)
+    q_ref[...] = result.astype(BF16)
+    for copy in sent:
+        copy.wait_send()
+
+
+def reduce_queries(n, features, updated):
+    rows, width = features.shape[1], updated.shape[1]
+    nz = n // LINE
+    dma = pltpu.SemaphoreType.DMA
+    vmem = pl.BlockSpec(memory_space=pltpu.VMEM)
+    return pl.pallas_call(
+        functools.partial(reduce_kernel, n),
+        out_shape=jax.ShapeDtypeStruct((rows, width), BF16),
+        in_specs=[vmem] * 2,
+        out_specs=vmem,
+        scratch_shapes=[pltpu.VMEM((2 * nz, rows, width), BF16)] * 2
+        + [pltpu.VMEM((nz, rows, width), BF16)] * 4
+        + [pltpu.VMEM((nz, rows, width), F32)]
+        + [dma((2 * nz,))] * 2 + [dma((nz,))] * 4,
+        compiler_params=pltpu.CompilerParams(collective_id=1, has_side_effects=True),
+        name="reduce_queries",
+    )(features, updated)
+
 
 def body(inputs, out_grads, weights, left_stats, right_stats, left_roots, right_roots, refresh):
     tok_local, model_width = inputs.shape
@@ -53,12 +237,18 @@
     col_blocks = col_count // block
     replicas = lax.axis_size("dp")
     tok_total = tok_local * replicas
-    mine = lax.axis_index("dp") % col_blocks
-    grads = lax.all_gather(out_grads, "dp", axis=0, tiled=True)
-    grads = lax.dynamic_slice_in_dim(grads, mine * block, block, 1)
-    send = jnp.repeat(inputs.reshape(tok_local, row_blocks, block).transpose(1, 0, 2), col_blocks, axis=0)
-    features = lax.all_to_all(send, "dp", split_axis=0, concat_axis=0, tiled=True)
-    features = features.reshape(tok_total, block)
+    kernels = col_blocks == 1 and lax.axis_size("owner") == 2 and replicas % LINE == 0
+    if kernels:
+        features, grads = gather(replicas, inputs, out_grads)
+        features = features.reshape(tok_total, block)
+        grads = grads.reshape(tok_total, block)
+    else:
+        mine = lax.axis_index("dp") % col_blocks
+        grads = lax.all_gather(out_grads, "dp", axis=0, tiled=True)
+        grads = lax.dynamic_slice_in_dim(grads, mine * block, block, 1)
+        send = jnp.repeat(inputs.reshape(tok_local, row_blocks, block).transpose(1, 0, 2), col_blocks, axis=0)
+        features = lax.all_to_all(send, "dp", split_axis=0, concat_axis=0, tiled=True)
+        features = features.reshape(tok_total, block)
     gradient = dot(features, grads, ((0,), (0,))) / tok_total
     left_new = BETA * left_stats[0] + (1.0 - BETA) * dot(gradient, gradient, ((1,), (1,)))
     right_new = BETA * right_stats[0] + (1.0 - BETA) * dot(gradient, gradient, ((0,), (0,)))
@@ -69,10 +259,13 @@
     direction = direction * (block / jnp.sqrt(jnp.sum(direction * direction) + 1e-12))
     rate = 0.25 / math.sqrt(model_width)
     updated = (weights[0] - rate * direction).astype(BF16)
-    partial = dot(features, updated).astype(BF16)
-    if col_blocks > 1:
-        partial = lax.dynamic_update_slice(jnp.zeros((tok_total, col_count), BF16), partial, (0, mine * block))
-    queries = lax.psum_scatter(partial, "dp", scatter_dimension=0, tiled=True)
+    if kernels:
+        queries = reduce_queries(replicas, features.reshape(replicas, tok_local, block), updated)
+    else:
+        partial = dot(features, updated).astype(BF16)
+        if col_blocks > 1:
+            partial = lax.dynamic_update_slice(jnp.zeros((tok_total, col_count), BF16), partial, (0, mine * block))
+        queries = lax.psum_scatter(partial, "dp", scatter_dimension=0, tiled=True)
     return (left_new[None], right_new[None], left_root[None], right_root[None], direction[None], queries)
 
 

time: 188 us -> 121 us (0.64)
  waiting for transfers between devices: 120 us -> 0 us
  Pallas kernels: 0 us -> 85.8 us
  between operations: 15.5 us -> 2.1 us
  local copies, waits for them, and re-layouts: 19.5 us -> 9.77 us
  starting transfers between devices: 6.02 us -> 0 us
  matrix products: 21.1 us -> 18.7 us
    pallas_call x0 -> x2, Pallas kernels: none -> 85.8 us  [the longest x1 50.5 us: gather(): pl.pallas_call(functools.partial(gather_kernel, n), out_shape=[jax.ShapeD...]
    unnamed x3 -> x0, waiting for transfers between devices: 62.7 us -> none
    all_to_all x1 -> x0, waiting for transfers between devices: 43.8 us -> none  [body(): lax.all_to_all(send, 'dp', split_axis=0, concat_axis=0, tiled=True)]
    all_gather x1 -> x0, waiting for transfers between devices: 13.8 us -> none  [body(): grads = lax.all_gather(out_grads, 'dp', axis=0, tiled=True)]
    unnamed x31 -> x28, local copies, waits for them, and re-layouts: 16.9 us -> 9.77 us
    all_to_all x1 -> x0, starting transfers between devices: 5.94 us -> none  [body(): lax.all_to_all(send, 'dp', split_axis=0, concat_axis=0, tiled=True)]
    all_to_all x1 -> x0, local copies, waits for them, and re-layouts: 2.63 us -> none  [body(): lax.all_to_all(send, 'dp', split_axis=0, concat_axis=0, tiled=True)]
    dot_general x16 -> x15, matrix products: 21.1 us -> 18.7 us  [dot(): lax.dot_general(a.astype(BF16), b.astype(BF16), (dims, ((), ())), preferr...]
  transfers between devices with their start and end apart: 3 -> 0, of which waited for: 3 -> 0; matrix products, arithmetic and copies ran while one was open for 2% -> 0% of each run, Pallas kernels for 0% -> 0%
where the time goes in v2:
time: 121 us; the launch traced here: 120 us
  Pallas kernels  85.8 us (71%)
  matrix products  18.7 us (15%)
  local copies, waits for them, and re-layouts  9.77 us (8%)
  other arithmetic  2.37 us (2%)
  between operations  2.1 us (2%)
  loops' own time  1.74 us (1%)
    pallas_call x1, Pallas kernels, gather(): pl.pallas_call(functools.partial(gather_kernel, n), out_shape=[jax.ShapeD...  50.5 us
    pallas_call x1, Pallas kernels, reduce_queries(): pl.pallas_call(functools.partial(reduce_kernel, n), out_shape=jax.ShapeDt...  35.2 us
    dot_general x15, matrix products, dot(): lax.dot_general(a.astype(BF16), b.astype(BF16), (dims, ((), ())), preferr...  18.7 us
    unnamed x28, local copies, waits for them, and re-layouts  9.77 us

profile of v2, /device:TPU:2, one launch (start us, length us, event | category | flops | bytes accessed | tf_op | source)
XLA Modules:
  0.0 120.5 jit_solution(7635241800664563764)
XLA Ops:
  0.6 2.3 %copy.33 = f32[1,512,512]{2,1,0:T(8,128)} copy(f32[1,512,512]{2,1,0:T(8,128)} %param.16) | data formatting | bytes 2097152
  3.5 50.5 %gather_blocks.1 = (bf16[16,128,512]{2,1,0:T(8,128)(2,1)}, bf16[16,128,512]{2,1,0:T(8,128)(2,1)}) custom-call(bf16[128,8192]{1,0:T(8,128)(2,1)} %x_ref.1, bf16[128,512]{1,0:T(8,128)(2,1)} %g_ref.1), custom_call_target="tpu_custom_call" | custom-call | tf_op jit(solution)/shard_map/gather_blocks/pallas_call | solution.py:154
  54.1 0.0 copy-start.8
  54.1 4.6 %fusion.83 = (bf16[512,512]{1,0:T(8,128)(2,1)S(1)}, f32[512,512]{1,0:T(8,128)}) fusion(bf16[16,128,512]{2,1,0:T(8,128)(2,1)} %get-tuple-element.42.f_ref, bf16[16,128,512]{2,1,0:T(8,128)(2,1)} %get-tuple-element.43), kind=kOutput, calls=%fused_computation.102 | convolution fusion | flops 1074266112 | bytes 5767168 | tf_op jit(solution)/shard_map/dot_general | solution.py:18
  58.7 0.0 copy-start.9
  58.7 0.0 copy-done.8
  58.7 0.5 fusion.66
  59.2 0.0 copy-start.3
  59.2 0.0 copy-start.2
  59.2 0.7 copy-done.9
  59.9 0.5 fusion.67
  60.4 0.0 copy-start.4
  60.4 0.5 copy-done.2
  60.9 0.0 copy-done.3
  60.9 0.5 copy-done.4
  61.4 11.1 %conditional.2 = (f32[512,512]{1,0:T(8,128)S(1)}, f32[512,512]{1,0:T(8,128)}, f32[1,512,512]{2,1,0:T(8,128)}, f32[1,512,512]{2,1,0:T(8,128)S(1)}) conditional(s32[]{:T(128)} %bitcast.9, (f32[1,512,512]{2,1,0:T(8,128)S(1)}, f32[1,512,512]{2,1,0:T(8,128)}) %tuple.53, (f32[512,512]{1,0:T(8,128)S(1)}, f32[512,512]{1,0:T(8,128)S(1)}) %tuple.31), branch_computations={%region_0.0_spmd.clone, %region_1.0_spmd.clone} | conditional | flops 1634729984 | bytes 46137628
  61.4 0.0 copy-start.5
  61.4 1.0 copy-done.5
  62.3 1.0 multiply_reduce_fusion
  63.3 0.0 copy-start.6
  65.0 0.5 fusion.16
  65.4 0.0 copy-done.6
  65.4 0.5 fusion.11
  65.9 0.0 copy-start.7
  65.9 0.5 fusion.3
  66.4 0.7 copy-done.7
  67.1 0.6 fusion.2
  67.7 0.0 copy-start
  67.7 1.0 copy.24
  68.7 0.5 fusion.1
  69.2 0.0 copy-done
  69.3 1.6 %fusion = f32[512,512]{1,0:T(8,128)} fusion(f32[512,512]{1,0:T(8,128)S(1)} %fusion.1, f32[512,512]{1,0:T(8,128)S(1)} %fusion.16, f32[512,512]{1,0:T(8,128)S(1)} %get-tuple-element.69, f32[]{:T(128)S(6)} %div.19, f32[]{:T(128)S(6)} %sqrt.27), kind=kOutput, calls=%fused_computation.5 | convolution fusion | flops 274202624 | bytes 4194312 | tf_op jit(solution)/shard_map/cond/branch_1_fun/dot_general | solution.py:18
  70.9 0.0 copy-start.1
  70.9 1.3 %copy.25 = f32[1,512,512]{2,1,0:T(8,128)S(1)} copy(f32[1,512,512]{2,1,0:T(8,128)} %bitcast.15) | data formatting | bytes 2097152
  72.2 0.2 copy-done.1
  72.4 0.0 copy-start.10
  72.4 2.1 %fusion.70 = f32[512,512]{1,0:T(8,128)S(1)} fusion(f32[512,512]{1,0:T(8,128)} %get-tuple-element.79, bf16[512,512]{1,0:T(8,128)(2,1)S(1)} %get-tuple-element.78, f32[512,512]{1,0:T(8,128)S(1)} %get-tuple-element.60), kind=kOutput, calls=%fused_computation.89 | convolution fusion | flops 269484032 | bytes 3670016 | tf_op jit(solution)/shard_map/dot_general | solution.py:18
  74.5 0.0 copy-done.10
  74.5 0.4 fusion.77
  74.9 0.4 fusion.65
  75.4 2.0 %fusion.71 = f32[512,512]{1,0:T(8,128)S(1)} fusion(f32[512,512]{1,0:T(8,128)} %get-tuple-element.61, f32[512,512]{1,0:T(8,128)S(1)} %fusion.65), kind=kOutput, calls=%fused_computation.90 | convolution fusion | flops 269746176 | bytes 3145728 | tf_op jit(solution)/shard_map/dot_general | solution.py:18
  77.4 1.7 %fusion.73 = f32[512,512]{1,0:T(8,128)S(1)} fusion(f32[512,512]{1,0:T(8,128)} %get-tuple-element.61, f32[512,512]{1,0:T(8,128)S(1)} %fusion.65), kind=kOutput, calls=%fused_computation.92 | convolution fusion | flops 268959744 | bytes 3145728 | tf_op jit(solution)/shard_map/dot_general | solution.py:18
  79.0 0.0 copy-start.11
  79.1 2.5 %multiply_reduce_fusion.2 = (f32[]{:T(128)}, f32[512,512]{1,0:T(8,128)S(1)}) fusion(f32[512,512]{1,0:T(8,128)S(1)} %fusion.73, f32[512,512]{1,0:T(8,128)S(1)} %fusion.71, f32[512,512]{1,0:T(8,128)} %get-tuple-element.61, f32[512,512]{1,0:T(8,128)S(1)} %fusion.65), kind=kOutput, calls=%fused_computation.83 | convolution fusion | flops 270794752 | bytes 5242884 | tf_op jit(solution)/shard_map/dot_general | solution.py:18
  82.3 0.0 copy-done.11
  82.3 1.4 %fusion.69 = (bf16[512,512]{1,0:T(8,128)(2,1)}, f32[1,512,512]{2,1,0:T(8,128)}) fusion(f32[1,512,512]{2,1,0:T(8,128)S(1)} %copy-done.11, f32[512,512]{1,0:T(8,128)S(1)} %get-tuple-element.81, f32[]{:T(128)S(6)} %div.17), kind=kLoop, calls=%fused_computation.82 | loop fusion | flops 1048576 | bytes 3670020 | tf_op jit(solution)/shard_map/convert_element_type | solution.py:261
  83.7 35.2 %reduce_queries.1 = bf16[128,512]{1,0:T(8,128)(2,1)} custom-call(bf16[16,128,512]{2,1,0:T(8,128)(2,1)} %get-tuple-element.42.f_ref, bf16[512,512]{1,0:T(8,128)(2,1)} %get-tuple-element.76.w_ref), custom_call_target="tpu_custom_call" | custom-call | tf_op jit(solution)/shard_map/reduce_queries/pallas_call | solution.py:218
  118.9 1.6 %copy.34 = bf16[128,512]{1,0:T(8,128)(2,1)} copy(bf16[128,512]{1,0:T(8,128)(2,1)} %reduce_queries.1) | data formatting | bytes 262144
Async XLA Ops:
  54.1 4.6 %copy-start.8 = (f32[1,512,512]{2,1,0:T(8,128)S(1)}, f32[1,512,512]{2,1,0:T(8,128)}, u32[]{:S(2)}) copy-start(f32[1,512,512]{2,1,0:T(8,128)} %param.14) | copy-start | bytes 3145732
  58.7 1.2 %copy-start.9 = (f32[1,512,512]{2,1,0:T(8,128)S(1)}, f32[1,512,512]{2,1,0:T(8,128)}, u32[]{:S(2)}) copy-start(f32[1,512,512]{2,1,0:T(8,128)} %param.13) | copy-start | bytes 3145732
  59.2 1.7 %copy-start.3 = (f32[512,512]{1,0:T(8,128)}, f32[512,512]{1,0:T(8,128)S(1)}, u32[]{:S(2)}) copy-start(f32[512,512]{1,0:T(8,128)S(1)} %fusion.66) | copy-start | bytes 3145732
  59.2 1.7 %copy-start.2 = (f32[1,512,512]{2,1,0:T(8,128)S(1)}, f32[1,512,512]{2,1,0:T(8,128)}, u32[]{:S(2)}) copy-start(f32[1,512,512]{2,1,0:T(8,128)} %param.15) | copy-start | bytes 3145732
  60.4 1.0 copy-start.4
  61.4 1.0 copy-start.5
  63.3 2.1 %copy-start.6 = (f32[512,512]{1,0:T(8,128)S(1)}, f32[512,512]{1,0:T(8,128)}, u32[]{:S(2)}) copy-start(f32[512,512]{1,0:T(8,128)} %copy-done.5) | copy-start | bytes 3145732
  65.9 1.2 %copy-start.7 = (f32[512,512]{1,0:T(8,128)S(1)}, f32[512,512]{1,0:T(8,128)}, u32[]{:S(2)}) copy-start(f32[512,512]{1,0:T(8,128)} %copy-done.5) | copy-start | bytes 3145732
  67.7 1.5 %copy-start = (f32[512,512]{1,0:T(8,128)}, f32[512,512]{1,0:T(8,128)S(1)}, u32[]{:S(2)}) copy-start(f32[512,512]{1,0:T(8,128)S(1)} %fusion.2) | copy-start | bytes 3145732
  70.9 1.5 %copy-start.1 = (f32[512,512]{1,0:T(8,128)S(1)}, f32[512,512]{1,0:T(8,128)}, u32[]{:S(2)}) copy-start(f32[512,512]{1,0:T(8,128)} %copy-done) | copy-start | bytes 3145732
  72.4 2.1 %copy-start.10 = (f32[1,512,512]{2,1,0:T(8,128)}, f32[1,512,512]{2,1,0:T(8,128)S(1)}, u32[]{:S(2)}) copy-start(f32[1,512,512]{2,1,0:T(8,128)S(1)} %get-tuple-element.101) | copy-start | bytes 3145732
  79.0 3.2 %copy-start.11 = (f32[1,512,512]{2,1,0:T(8,128)S(1)}, f32[1,512,512]{2,1,0:T(8,128)}, u32[]{:S(2)}) copy-start(f32[1,512,512]{2,1,0:T(8,128)} %param.12) | copy-start | bytes 3145732
